TPU v7x, 32 devices: a whole 2x2x4 slice. The times are simulated.
32 devices in a mesh: dom: 8 (over z, y), rep: 4 (over x, core).
Axes of the slice: x: 2, y: 2, z: 4, core: 2. Of those that a mesh axis runs over, the one named last changes fastest.
Arguments:
- embedding: float32 [4096, 400], P('dom'), may hold values from -1.5 to 1.5
- adagrad_sum: float32 [4096], P('dom'), may hold values from 0.01 to 1
- row_lists: int32 [4, 8, 8, 16], P('rep', 'dom'), may hold values from 0 to 511, as said below
- source_slots: int32 [4, 8, 2, 512], P('rep', 'dom'), may hold values from 0 to 127, as said below
- target_slots: int32 [4, 8, 2, 512], P('rep', 'dom'), may hold values from 0 to 127, as said below
- negative_ids: int32 [4, 8, 2, 2, 512], P('rep', 'dom'), may hold values from 0 to 511
Outputs:
- new_embedding: float32 [4096, 400], P('dom')
- new_adagrad_sum: float32 [4096], P('dom')
Inputs may be any that keep to these rules, and one draw needn't show every extreme that they name: `row_lists`: for each worker and owner, a count of leading entries are distinct rows of that owner and the other entries are 0. For the worker with index w along dom, the owners (w + c) mod 8, c < 4, have all 16 entries live; every other owner has 1 to 8 live entries. `source_slots`: every slot named is among the leading live entries of the worker's row list for its owner; entries k >= 8 are named only for the owners (w + c) mod 8, c < 4, of the worker with index w along dom. `target_slots`: every slot named is among the leading live entries of the worker's row list for its owner; entries k >= 8 are named only for the owners (w + c) mod 8, c < 4, of the worker with index w along dom.
All inputs are finite; a program needn't handle non-finite values.
Results may differ from a plain program's by a relative error of at most 0.0003.
Values sent between devices are 32-bit elements; how exact they have to be, the bound alone decides.
A program may use at most 64 MiB of HBM per device.

v0:
```python
import jax
import jax.numpy as jnp
from jax import lax
from jax.sharding import PartitionSpec as P

learn_rate = 0.1


def batch_grads(buffer, sources, targets, neg_dst, neg_src):
    highest = lax.Precision.HIGHEST
    src_rows = buffer[sources]
    dst_rows = buffer[targets]
    neg_dst_rows = buffer[targets[neg_dst]]
    neg_src_rows = buffer[sources[neg_src]]
    samples = neg_dst.shape[0]
    positive = jnp.sum(src_rows * dst_rows, axis=1)
    pos_weight = -jax.nn.sigmoid(-positive)[:, None]
    dst_scores = jnp.dot(src_rows, neg_dst_rows.T, precision=highest)
    src_scores = jnp.dot(dst_rows, neg_src_rows.T, precision=highest)
    dst_weight = jax.nn.sigmoid(dst_scores) / samples
    src_weight = jax.nn.sigmoid(src_scores) / samples
    grad_src = pos_weight * dst_rows + jnp.dot(dst_weight, neg_dst_rows, precision=highest)
    grad_dst = pos_weight * src_rows + jnp.dot(src_weight, neg_src_rows, precision=highest)
    grad_negd = jnp.dot(dst_weight.T, src_rows, precision=highest)
    grad_negs = jnp.dot(src_weight.T, dst_rows, precision=highest)
    gradient = jnp.zeros(buffer.shape, buffer.dtype)
    gradient = gradient.at[sources].add(grad_src).at[targets].add(grad_dst)
    gradient = gradient.at[targets[neg_dst]].add(grad_negd).at[sources[neg_src]].add(grad_negs)
    return gradient


def all_batches(buffer, sources, targets, negatives):
    gradient = jnp.zeros(buffer.shape, buffer.dtype)
    for batch in range(sources.shape[0]):
        gradient = gradient + batch_grads(
            buffer, sources[batch], targets[batch], negatives[batch, 0], negatives[batch, 1]
        )
    return gradient


def adagrad(rows_now, sum_now, row_grad):
    new_sum = sum_now + jnp.mean(row_grad * row_grad, axis=1)
    new_rows = rows_now - learn_rate * row_grad / jnp.sqrt(new_sum)[:, None]
    return (new_rows, new_sum)


def local(embedding, adagrad_sum, row_lists, source_slots, target_slots, negative_ids):
    requests = row_lists[0, 0]
    owners, capacity = requests.shape
    width = embedding.shape[1]
    sources = source_slots[0, 0]
    targets = target_slots[0, 0]
    negatives = negative_ids[0, 0]
    incoming = lax.all_to_all(requests, "dom", split_axis=0, concat_axis=0, tiled=True)
    owned_sum = jnp.zeros(embedding.shape, jnp.float32)
    pulled = lax.all_to_all(embedding[incoming], "dom", split_axis=0, concat_axis=0, tiled=True)
    buffer = pulled.reshape(owners * capacity, width)
    gradient = all_batches(buffer, sources, targets, negatives)
    returned = lax.all_to_all(
        gradient.reshape(owners, capacity, width), "dom", split_axis=0, concat_axis=0, tiled=True
    )
    owned_sum = owned_sum.at[incoming.reshape(-1)].add(returned.reshape(-1, width))
    summed = lax.psum(owned_sum, "rep")
    return adagrad(embedding, adagrad_sum, summed)


def solution(mesh):
    in_specs = (
        P("dom", None),
        P("dom"),
        P("rep", "dom", None, None),
        P("rep", "dom", None, None),
        P("rep", "dom", None, None),
        P("rep", "dom", None, None, None),
    )
    out_specs = (P("dom", None), P("dom"))
    return jax.shard_map(local, mesh=mesh, in_specs=in_specs, out_specs=out_specs, check_vma=False)
```

profile of v0, /device:TPU:0, one launch (start us, length us, event | category | flops | bytes accessed | tf_op | source)
XLA Modules:
  0.0 193.2 jit_solution(12102524834841163273)
XLA Ops:
  7.2 7.3 %all-to-all-start = ((s32[8,1,16]{2,1,0:T(1,128)}), s32[8,1,16]{2,1,0:T(1,128)S(1)}, u32[]{:S(2)}, u32[]{:S(2)}) async-start(s32[8,1,16]{2,1,0:T(1,128)} %bitcast.120), calls=%async_computation | async-start | bytes 8192 | tf_op jit(solution)/shard_map/all_to_all | solution.py:54
  15.9 3.5 %gather_fusion.3 = s32[512]{0:T(512)S(1)} fusion(s32[512]{0:T(512)S(1)} %bitcast.91, s32[1024]{0:T(1024)S(1)} %pad_clamp_fusion.9), kind=kCustom, calls=%fused_computation.3 | custom fusion | bytes 6144 | tf_op jit(solution)/shard_map/gather | solution.py:13
  19.5 3.5 %gather_fusion.5 = s32[512]{0:T(512)S(1)} fusion(s32[512]{0:T(512)S(1)} %bitcast.92, s32[1024]{0:T(1024)S(1)} %pad_clamp_fusion.7), kind=kCustom, calls=%fused_computation.5 | custom fusion | bytes 6144 | tf_op jit(solution)/shard_map/gather | solution.py:14
  23.1 3.5 %gather_fusion.9 = s32[512]{0:T(512)S(1)} fusion(s32[512]{0:T(512)S(1)} %bitcast.90, s32[1024]{0:T(1024)S(1)} %pad_clamp_fusion.3), kind=kCustom, calls=%fused_computation.9 | custom fusion | bytes 6144 | tf_op jit(solution)/shard_map/gather | solution.py:13
  27.1 1.5 gather_fusion
  28.5 6.2 %all-to-all-start.1 = ((f32[8,16,400]{2,1,0:T(8,128)}), f32[8,16,400]{2,1,0:T(8,128)S(1)}, u32[]{:S(2)}, u32[]{:S(2)}) async-start(f32[8,16,400]{2,1,0:T(8,128)} %bitcast.6), calls=%async_computation.1 | async-start | bytes 524288 | tf_op jit(solution)/shard_map/all_to_all | solution.py:56
  34.7 3.5 %gather_fusion.11 = s32[512]{0:T(512)S(1)} fusion(s32[512]{0:T(512)S(1)} %bitcast.89, s32[1024]{0:T(1024)S(1)} %pad_clamp_fusion.1), kind=kCustom, calls=%fused_computation.11 | custom fusion | bytes 6144 | tf_op jit(solution)/shard_map/gather | solution.py:14
  38.3 4.9 %all-to-all-done.1 = f32[8,16,400]{2,1,0:T(8,128)S(1)} async-done(((f32[8,16,400]{2,1,0:T(8,128)}), f32[8,16,400]{2,1,0:T(8,128)S(1)}, u32[]{:S(2)}, u32[]{:S(2)}) %all-to-all-start.1) | async-done | bytes 204832 | tf_op jit(solution)/shard_map/all_to_all | solution.py:56
  43.2 1.6 gather_fusion.1
  44.8 1.6 gather_fusion.2
  46.4 1.2 copy.30
  47.8 1.2 copy.32
  49.1 1.6 gather_fusion.7
  50.7 1.6 gather_fusion.8
  52.3 1.2 copy.36
  53.7 1.2 copy.38
  54.9 2.3 %gather_fusion.4 = f32[512,400]{1,0:T(8,128)} fusion(f32[128,400]{1,0:T(8,128)S(1)} %bitcast.85, s32[1024]{0:T(1024)S(1)} %pad_clamp_fusion.8), kind=kCustom, calls=%fused_computation.4 | custom fusion | bytes 1640448 | tf_op jit(solution)/shard_map/gather | solution.py:13
  57.2 3.6 %fusion.15 = f32[512,512]{1,0:T(8,128)S(1)} fusion(f32[512,400]{1,0:T(8,128)} %copy-done, f32[512,400]{1,0:T(8,128)} %gather_fusion.4), kind=kOutput, calls=%fused_computation.41 | convolution fusion | flops 1259339776 | bytes 2686976 | tf_op jit(solution)/shard_map/dot_general | solution.py:18
  60.9 2.9 %fusion.26 = f32[512,400]{1,0:T(8,128)} fusion(f32[512,512]{1,0:T(8,128)S(1)} %fusion.15, f32[512,400]{1,0:T(8,128)S(1)} %copy-done.1), kind=kOutput, calls=%fused_computation.94 | convolution fusion | flops 1258291200 | bytes 2686976 | tf_op jit(solution)/shard_map/dot_general | solution.py:24
  63.8 3.0 %convolution_add_fusion.3 = f32[512,400]{0,1:T(8,128)} fusion(f32[512,512]{1,0:T(8,128)S(1)} %fusion.15, f32[512,400]{1,0:T(8,128)S(1)} %copy-done.8, f32[512,400]{0,1:T(8,128)S(1)} %copy-done.15, f32[512]{0:T(512)S(1)} %divide_negate_fusion.1), kind=kOutput, calls=%fused_computation.45 | convolution fusion | flops 1258700800 | bytes 3508224 | tf_op jit(solution)/shard_map/dot_general | solution.py:22
  66.8 2.5 %copy.31 = f32[512,400]{1,0:T(8,128)} copy(f32[512,400]{0,1:T(8,128)} %convolution_add_fusion.3) | data formatting | bytes 1638400 | tf_op jit(solution)/shard_map/add | solution.py:22
  69.2 2.5 %gather_fusion.6 = f32[512,400]{1,0:T(8,128)} fusion(f32[128,400]{1,0:T(8,128)S(1)} %bitcast.86, s32[1024]{0:T(1024)S(1)} %pad_clamp_fusion.6), kind=kCustom, calls=%fused_computation.6 | custom fusion | bytes 1640448 | tf_op jit(solution)/shard_map/gather | solution.py:14
  71.8 3.2 %fusion.11 = f32[512,512]{1,0:T(8,128)S(1)} fusion(f32[512,400]{1,0:T(8,128)S(1)} %gather_fusion.2, f32[512,400]{1,0:T(8,128)} %gather_fusion.6), kind=kOutput, calls=%fused_computation.36 | convolution fusion | flops 1259339776 | bytes 2686976 | tf_op jit(solution)/shard_map/dot_general | solution.py:19
  75.0 2.8 %fusion.27 = f32[512,400]{1,0:T(8,128)} fusion(f32[512,512]{1,0:T(8,128)S(1)} %fusion.11, f32[512,400]{1,0:T(8,128)S(1)} %gather_fusion.2), kind=kOutput, calls=%fused_computation.95 | convolution fusion | flops 1258291200 | bytes 2686976 | tf_op jit(solution)/shard_map/dot_general | solution.py:25
  77.9 2.1 %convolution_add_fusion.2 = f32[512,400]{0,1:T(8,128)S(1)} fusion(f32[512,512]{1,0:T(8,128)S(1)} %fusion.11, f32[512,400]{1,0:T(8,128)S(1)} %copy-done.9, f32[512,400]{0,1:T(8,128)S(1)} %copy-done.14, f32[512]{0:T(512)S(1)} %divide_negate_fusion.1), kind=kOutput, calls=%fused_computation.44 | convolution fusion | flops 1258700800 | bytes 3508224 | tf_op jit(solution)/shard_map/dot_general | solution.py:23
  80.0 1.4 copy.33
  81.4 2.0 %gather_fusion.10 = f32[512,400]{1,0:T(8,128)S(1)} fusion(f32[128,400]{1,0:T(8,128)S(1)} %bitcast.87, s32[1024]{0:T(1024)S(1)} %pad_clamp_fusion.2), kind=kCustom, calls=%fused_computation.10 | custom fusion | bytes 1640448 | tf_op jit(solution)/shard_map/gather | solution.py:13
  83.4 2.0 %fusion.7 = f32[512,512]{1,0:T(8,128)S(1)} fusion(f32[512,400]{1,0:T(8,128)S(1)} %gather_fusion.7, f32[512,400]{1,0:T(8,128)S(1)} %gather_fusion.10), kind=kOutput, calls=%fused_computation.31 | convolution fusion | flops 1259339776 | bytes 2686976 | tf_op jit(solution)/shard_map/dot_general | solution.py:18
  85.4 2.8 %fusion.28 = f32[512,400]{1,0:T(8,128)} fusion(f32[512,512]{1,0:T(8,128)S(1)} %fusion.7, f32[512,400]{1,0:T(8,128)S(1)} %gather_fusion.7), kind=kOutput, calls=%fused_computation.96 | convolution fusion | flops 1258291200 | bytes 2686976 | tf_op jit(solution)/shard_map/dot_general | solution.py:24
  88.3 2.1 %convolution_add_fusion.1 = f32[512,400]{0,1:T(8,128)S(1)} fusion(f32[512,512]{1,0:T(8,128)S(1)} %fusion.7, f32[512,400]{1,0:T(8,128)S(1)} %gather_fusion.10, f32[512,400]{0,1:T(8,128)S(1)} %copy-done.13, f32[512]{0:T(512)S(1)} %divide_negate_fusion), kind=kOutput, calls=%fused_computation.43 | convolution fusion | flops 1258700800 | bytes 3508224 | tf_op jit(solution)/shard_map/dot_general | solution.py:22
  90.7 4.3 %scatter_custom_fusion = f32[128,400]{1,0:T(8,128)S(1)} fusion(s32[512]{0:T(512)S(1)} %bitcast.111, f32[512,400]{1,0:T(8,128)} %copy.31, f32[]{:T(128)} %constant.8.clone.1), kind=kCustom, calls=%fused_computation.54 | custom fusion | flops 204800 | bytes 205312 | tf_op jit(solution)/shard_map/scatter-add | solution.py:27
  95.0 3.6 %scatter_custom_fusion.4 = f32[128,400]{1,0:T(8,128)S(1)} fusion(s32[512]{0:T(512)S(1)} %bitcast.109, f32[512,400]{1,0:T(8,128)S(1)} %copy.37, f32[]{:T(128)} %constant.8.clone.1), kind=kCustom, calls=%fused_computation.52 | custom fusion | flops 204800 | bytes 204804 | tf_op jit(solution)/shard_map/scatter-add | solution.py:27
  98.7 1.8 gather_fusion.12
  100.5 2.0 %fusion.3 = f32[512,512]{1,0:T(8,128)S(1)} fusion(f32[512,400]{1,0:T(8,128)S(1)} %gather_fusion.8, f32[512,400]{1,0:T(8,128)S(1)} %gather_fusion.12), kind=kOutput, calls=%fused_computation.26 | convolution fusion | flops 1259339776 | bytes 2686976 | tf_op jit(solution)/shard_map/dot_general | solution.py:19
  102.5 2.8 %fusion.29 = f32[512,400]{1,0:T(8,128)} fusion(f32[512,512]{1,0:T(8,128)S(1)} %fusion.3, f32[512,400]{1,0:T(8,128)S(1)} %gather_fusion.8), kind=kOutput, calls=%fused_computation.97 | convolution fusion | flops 1258291200 | bytes 2686976 | tf_op jit(solution)/shard_map/dot_general | solution.py:25
  105.4 2.1 %convolution_add_fusion = f32[512,400]{0,1:T(8,128)S(1)} fusion(f32[512,512]{1,0:T(8,128)S(1)} %fusion.3, f32[512,400]{1,0:T(8,128)S(1)} %gather_fusion.12, f32[512,400]{0,1:T(8,128)S(1)} %copy-done.12, f32[512]{0:T(512)S(1)} %divide_negate_fusion), kind=kOutput, calls=%fused_computation.42 | convolution fusion | flops 1258700800 | bytes 3508224 | tf_op jit(solution)/shard_map/dot_general | solution.py:23
  107.5 1.3 copy.39
  108.8 3.7 %scatter_fusion = f32[128,400]{1,0:T(8,128)S(1)} fusion(f32[128,400]{1,0:T(8,128)S(1)} %scatter_custom_fusion, s32[512]{0:T(512)S(1)} %bitcast.106, f32[512,400]{1,0:T(8,128)S(1)} %copy-done.10), kind=kCustom, calls=%fused_computation.14 | custom fusion | flops 204800 | bytes 2459648 | tf_op jit(solution)/shard_map/scatter-add | solution.py:27
  112.5 3.7 %scatter_fusion.1 = f32[128,400]{1,0:T(8,128)S(1)} fusion(f32[128,400]{1,0:T(8,128)S(1)} %scatter_fusion, s32[512]{0:T(512)S(1)} %bitcast.96, f32[512,400]{1,0:T(8,128)S(1)} %copy-done.4), kind=kCustom, calls=%fused_computation.15 | custom fusion | flops 204800 | bytes 2459648 | tf_op jit(solution)/shard_map/scatter-add | solution.py:28
  116.3 3.9 %scatter_fusion.2 = f32[128,400]{1,0:T(8,128)S(1)} fusion(f32[128,400]{1,0:T(8,128)S(1)} %scatter_fusion.1, s32[512]{0:T(512)S(1)} %bitcast.98, f32[512,400]{1,0:T(8,128)S(1)} %copy-done.5), kind=kCustom, calls=%fused_computation.16 | custom fusion | flops 204800 | bytes 2459648 | tf_op jit(solution)/shard_map/scatter-add | solution.py:28
  120.2 4.5 %scatter_fusion.3 = f32[128,400]{1,0:T(8,128)S(1)} fusion(f32[128,400]{1,0:T(8,128)S(1)} %scatter_custom_fusion.4, s32[512]{0:T(512)S(1)} %bitcast.104, f32[512,400]{1,0:T(8,128)} %copy.39), kind=kCustom, calls=%fused_computation.18 | custom fusion | flops 204800 | bytes 2459648 | tf_op jit(solution)/shard_map/scatter-add | solution.py:27
  124.7 3.7 %scatter_fusion.4 = f32[128,400]{1,0:T(8,128)S(1)} fusion(f32[128,400]{1,0:T(8,128)S(1)} %scatter_fusion.3, s32[512]{0:T(512)S(1)} %bitcast.100, f32[512,400]{1,0:T(8,128)S(1)} %copy-done.6), kind=kCustom, calls=%fused_computation.19 | custom fusion | flops 204800 | bytes 2459648 | tf_op jit(solution)/shard_map/scatter-add | solution.py:28
  128.4 3.7 %scatter_fusion.5 = f32[128,400]{1,0:T(8,128)S(1)} fusion(f32[128,400]{1,0:T(8,128)S(1)} %scatter_fusion.4, s32[512]{0:T(512)S(1)} %bitcast.102, f32[512,400]{1,0:T(8,128)S(1)} %copy-done.7), kind=kCustom, calls=%fused_computation.20 | custom fusion | flops 204800 | bytes 2459648 | tf_op jit(solution)/shard_map/scatter-add | solution.py:28
  132.9 3.4 %all-to-all-start.2 = ((f32[8,16,400]{2,1,0:T(8,128)}), f32[8,16,400]{2,1,0:T(8,128)S(1)}, u32[]{:S(2)}, u32[]{:S(2)}) async-start(f32[8,16,400]{2,1,0:T(8,128)} %bitcast.35), calls=%async_computation.2 | async-start | bytes 524288 | tf_op jit(solution)/shard_map/all_to_all | solution.py:59
  137.7 7.2 %all-to-all-done.2 = f32[8,16,400]{2,1,0:T(8,128)S(1)} async-done(((f32[8,16,400]{2,1,0:T(8,128)}), f32[8,16,400]{2,1,0:T(8,128)S(1)}, u32[]{:S(2)}, u32[]{:S(2)}) %all-to-all-start.2) | async-done | bytes 204832 | tf_op jit(solution)/shard_map/all_to_all | solution.py:59
  144.9 2.3 %scatter_custom_fusion.8 = f32[512,400]{1,0:T(8,128)} fusion(s32[128]{0:T(128)S(1)} %fusion.22, f32[128,400]{1,0:T(8,128)S(1)} %bitcast.93, f32[]{:T(128)} %constant.8.clone.1), kind=kCustom, calls=%fused_computation.50 | custom fusion | flops 51200 | bytes 819204 | tf_op jit(solution)/shard_map/scatter-add | solution.py:62
  147.2 35.4 %all-reduce.2.cloned.1.call-done = f32[512,400]{1,0:T(8,128)} async-done(((f32[512,400]{1,0:T(8,128)}), f32[512,400]{1,0:T(8,128)}) %all-reduce.2.cloned.1.call-update) | async-done | bytes 819216 | tf_op jit(solution)/shard_map/psum | solution.py:63
  182.7 1.5 multiply_reduce_fusion
  (83 shorter events, 6.7 us)
Async XLA Ops:
  7.2 7.3 %copy-start.17 = (s32[1,1,2,512]{3,2,1,0:T(2,128)S(1)}, s32[1,1,2,512]{3,2,1,0:T(2,128)}, u32[]{:S(2)}) copy-start(s32[1,1,2,512]{3,2,1,0:T(2,128)} %param.10) | copy-start | bytes 12292
  7.2 19.8 %all-to-all-start = ((s32[8,1,16]{2,1,0:T(1,128)}), s32[8,1,16]{2,1,0:T(1,128)S(1)}, u32[]{:S(2)}, u32[]{:S(2)}) async-start(s32[8,1,16]{2,1,0:T(1,128)} %bitcast.120), calls=%async_computation | async-start | bytes 8192 | tf_op jit(solution)/shard_map/all_to_all | solution.py:54
  14.5 0.7 copy-start.18
  15.2 0.7 copy-start.19
  23.0 3.6 %copy-start.16 = (f32[512,400]{0,1:T(8,128)S(1)}, f32[512,400]{0,1:T(8,128)}, u32[]{:S(2)}) copy-start(f32[512,400]{0,1:T(8,128)} %param.6) | copy-start | bytes 2457604
  26.9 1.6 copy-start.2
  28.5 14.7 %all-to-all-start.1 = ((f32[8,16,400]{2,1,0:T(8,128)}), f32[8,16,400]{2,1,0:T(8,128)S(1)}, u32[]{:S(2)}, u32[]{:S(2)}) async-start(f32[8,16,400]{2,1,0:T(8,128)} %bitcast.6), calls=%async_computation.1 | async-start | bytes 524288 | tf_op jit(solution)/shard_map/all_to_all | solution.py:56
  44.8 3.0 %copy-start = (f32[512,400]{1,0:T(8,128)}, f32[512,400]{1,0:T(8,128)S(1)}, u32[]{:S(2)}) copy-start(f32[512,400]{1,0:T(8,128)S(1)} %gather_fusion.1) | copy-start | bytes 2457604
  57.2 3.6 %copy-start.1 = (f32[512,400]{1,0:T(8,128)S(1)}, f32[512,400]{1,0:T(8,128)}, u32[]{:S(2)}) copy-start(f32[512,400]{1,0:T(8,128)} %copy-done) | copy-start | bytes 2457604
  60.9 2.9 %copy-start.8 = (f32[512,400]{1,0:T(8,128)S(1)}, f32[512,400]{1,0:T(8,128)}, u32[]{:S(2)}) copy-start(f32[512,400]{1,0:T(8,128)} %gather_fusion.4) | copy-start | bytes 2457604
  60.9 2.9 %copy-start.15 = (f32[512,400]{0,1:T(8,128)S(1)}, f32[512,400]{0,1:T(8,128)}, u32[]{:S(2)}) copy-start(f32[512,400]{0,1:T(8,128)} %copy.30) | copy-start | bytes 2457604
  75.0 2.9 %copy-start.9 = (f32[512,400]{1,0:T(8,128)S(1)}, f32[512,400]{1,0:T(8,128)}, u32[]{:S(2)}) copy-start(f32[512,400]{1,0:T(8,128)} %gather_fusion.6) | copy-start | bytes 2457604
  75.0 2.9 %copy-start.14 = (f32[512,400]{0,1:T(8,128)S(1)}, f32[512,400]{0,1:T(8,128)}, u32[]{:S(2)}) copy-start(f32[512,400]{0,1:T(8,128)} %copy.32) | copy-start | bytes 2457604
  85.4 2.9 %copy-start.13 = (f32[512,400]{0,1:T(8,128)S(1)}, f32[512,400]{0,1:T(8,128)}, u32[]{:S(2)}) copy-start(f32[512,400]{0,1:T(8,128)} %copy.36) | copy-start | bytes 2457604
  102.5 2.9 %copy-start.12 = (f32[512,400]{0,1:T(8,128)S(1)}, f32[512,400]{0,1:T(8,128)}, u32[]{:S(2)}) copy-start(f32[512,400]{0,1:T(8,128)} %copy.38) | copy-start | bytes 2457604
  107.4 1.4 copy-start.10
  108.8 3.7 %copy-start.4 = (f32[512,400]{1,0:T(8,128)S(1)}, f32[512,400]{1,0:T(8,128)}, u32[]{:S(2)}) copy-start(f32[512,400]{1,0:T(8,128)} %fusion.26) | copy-start | bytes 2457604
  112.5 3.7 %copy-start.5 = (f32[512,400]{1,0:T(8,128)S(1)}, f32[512,400]{1,0:T(8,128)}, u32[]{:S(2)}) copy-start(f32[512,400]{1,0:T(8,128)} %fusion.27) | copy-start | bytes 2457604
  120.2 4.5 %copy-start.6 = (f32[512,400]{1,0:T(8,128)S(1)}, f32[512,400]{1,0:T(8,128)}, u32[]{:S(2)}) copy-start(f32[512,400]{1,0:T(8,128)} %fusion.28) | copy-start | bytes 2457604
  124.7 3.7 %copy-start.7 = (f32[512,400]{1,0:T(8,128)S(1)}, f32[512,400]{1,0:T(8,128)}, u32[]{:S(2)}) copy-start(f32[512,400]{1,0:T(8,128)} %fusion.29) | copy-start | bytes 2457604
  132.9 12.0 %all-to-all-start.2 = ((f32[8,16,400]{2,1,0:T(8,128)}), f32[8,16,400]{2,1,0:T(8,128)S(1)}, u32[]{:S(2)}, u32[]{:S(2)}) async-start(f32[8,16,400]{2,1,0:T(8,128)} %bitcast.35), calls=%async_computation.2 | async-start | bytes 524288 | tf_op jit(solution)/shard_map/all_to_all | solution.py:59
  136.3 46.3 %all-reduce.2.cloned.1.call-start = ((), (), s32[]{:S(2)}) async-start(), calls=%async_computation.3 | async-start | bytes 2097152 | tf_op jit(solution)/shard_map/psum | solution.py:63
  147.2 37.5 %copy-start.3 = (f32[512,400]{1,0:T(8,128)S(1)}, f32[512,400]{1,0:T(8,128)}, u32[]{:S(2)}) copy-start(f32[512,400]{1,0:T(8,128)} %copy-done.2) | copy-start | bytes 2457604
  147.2 36.9 %copy-start.20 = (f32[512]{0:T(512)S(1)}, f32[512]{0:T(512)}, u32[]{:S(2)}) copy-start(f32[512]{0:T(512)} %param.7) | copy-start | bytes 6148
  182.7 2.1 %copy-start.11 = (f32[512,400]{1,0:T(8,128)S(1)}, f32[512,400]{1,0:T(8,128)}, u32[]{:S(2)}) copy-start(f32[512,400]{1,0:T(8,128)} %all-reduce.2.cloned.1.call-done) | copy-start | bytes 2457604
Sparse Core Ops, SparseCore 0:
  147.3 35.2 all-reduce.1
where the time goes:
time: 196 us; the launch traced here: 193 us
  waiting for transfers between devices  47.6 us (24%)
  local copies, waits for them, and re-layouts  44.5 us (23%)
  other arithmetic  37.7 us (19%)
  matrix products  31.6 us (16%)
  starting transfers between devices  17 us (9%)
  between operations  14.9 us (8%)
    psum x1, waiting for transfers between devices, local(): summed = lax.psum(owned_sum, 'rep')  35.4 us
    scatter-add x4, other arithmetic, batch_grads(): gradient = gradient.at[sources].add(grad_src).at[targets].add(grad_dst)  16.1 us
    scatter-add x4, other arithmetic, batch_grads(): gradient.at[targets[neg_dst]].add(grad_negd).at[sources[neg_src]]  15.1 us
    gather x4, local copies, waits for them, and re-layouts, batch_grads(): neg_dst_rows = buffer[targets[neg_dst]]  11.3 us
    gather x4, local copies, waits for them, and re-layouts, batch_grads(): neg_src_rows = buffer[sources[neg_src]]  11.3 us
    all_to_all x1, starting transfers between devices, local(): lax.all_to_all(requests, 'dom', split_axis=0, concat_axis=0, tiled=True)  7.32 us
    all_to_all x1, waiting for transfers between devices, local(): lax.all_to_all(gradient.reshape(owners, capacity, width), 'dom', split_ax...  7.22 us
    all_to_all x1, starting transfers between devices, local(): lax.all_to_all(embedding[incoming], 'dom', split_axis=0, concat_axis=0, t...  6.19 us
  transfers between devices with their start and end apart: 4, of which 3 were waited for; matrix products, arithmetic and copies ran while one was open for 8% of the time, Pallas kernels for 0%

commit v1 on v0

v1 whole, which is shorter than its diff:
```python
import jax
import jax.numpy as jnp
from jax import lax
from jax.sharding import PartitionSpec as P

learn_rate = 0.1
HI = lax.Precision.HIGHEST


def slot_gradient(buffer, sources, targets, negatives):
    slots = buffer.shape[0]
    samples = negatives.shape[2]
    edges = sources.shape[1]
    ids = jnp.arange(slots, dtype=jnp.int32)
    src_hot = (sources[:, :, None] == ids).astype(jnp.float32)
    dst_hot = (targets[:, :, None] == ids).astype(jnp.float32)
    times = jnp.sum((negatives[:, :, :, None] == jnp.arange(edges, dtype=jnp.int32)).astype(jnp.float32), axis=2)
    cs = jnp.sum(src_hot, axis=1)
    ct = jnp.sum(dst_hot, axis=1)
    cp = jnp.sum(times[:, 0, :, None] * dst_hot, axis=1)
    cq = jnp.sum(times[:, 1, :, None] * src_hot, axis=1)
    pairs = jnp.sum(cs[:, :, None] * cp[:, None, :] + ct[:, :, None] * cq[:, None, :], axis=0)
    flat = (-1, slots)
    counts = lax.dot_general(
        src_hot.reshape(flat).astype(jnp.bfloat16), dst_hot.reshape(flat).astype(jnp.bfloat16),
        (((0,), (0,)), ((), ())), preferred_element_type=jnp.float32,
    )
    gram = jnp.dot(buffer, buffer.T, precision=HI)
    mixed = pairs * (jax.nn.sigmoid(gram) / samples) - counts * jax.nn.sigmoid(-gram)
    return jnp.dot(mixed + mixed.T, buffer, precision=HI)


def adagrad(rows_now, sum_now, row_grad):
    new_sum = sum_now + jnp.mean(row_grad * row_grad, axis=1)
    new_rows = rows_now - learn_rate * row_grad / jnp.sqrt(new_sum)[:, None]
    return (new_rows, new_sum)


def local(embedding, adagrad_sum, row_lists, source_slots, target_slots, negative_ids):
    requests = row_lists[0, 0]
    owners, capacity = requests.shape
    rows, width = embedding.shape
    incoming = lax.all_to_all(requests, "dom", split_axis=0, concat_axis=0, tiled=True)
    wanted = (incoming.reshape(-1)[:, None] == jnp.arange(rows, dtype=jnp.int32)).astype(jnp.float32)
    picked = jnp.dot(wanted, embedding, precision=HI).reshape(owners, capacity, width)
    pulled = lax.all_to_all(picked, "dom", split_axis=0, concat_axis=0, tiled=True)
    buffer = pulled.reshape(owners * capacity, width)
    gradient = slot_gradient(buffer, source_slots[0, 0], target_slots[0, 0], negative_ids[0, 0])
    returned = lax.all_to_all(
        gradient.reshape(owners, capacity, width), "dom", split_axis=0, concat_axis=0, tiled=True
    )
    owned = lax.dot_general(wanted, returned.reshape(-1, width), (((0,), (0,)), ((), ())), precision=HI)
    summed = lax.psum(owned, "rep")
    return adagrad(embedding, adagrad_sum, summed)


def solution(mesh):
    in_specs = (
        P("dom", None),
        P("dom"),
        P("rep", "dom", None, None),
        P("rep", "dom", None, None),
        P("rep", "dom", None, None),
        P("rep", "dom", None, None, None),
    )
    out_specs = (P("dom", None), P("dom"))
    return jax.shard_map(local, mesh=mesh, in_specs=in_specs, out_specs=out_specs, check_vma=False)
```

time: 196 us -> 94.4 us (0.48); the launches traced: 193 us -> 93.9 us
  local copies, waits for them, and re-layouts: 44.5 us -> 2.25 us
  other arithmetic: 37.7 us -> 5.75 us
  matrix products: 31.6 us -> 5.25 us
  blocking collectives: 0 us -> 11.1 us
  starting transfers between devices: 17 us -> 10.8 us
  waiting for transfers between devices: 47.6 us -> 44.6 us
    gather x17 -> x0, local copies, waits for them, and re-layouts: 35.4 us -> none  [the longest x4 11.3 us: batch_grads(): neg_dst_rows = buffer[targets[neg_dst]]]
    scatter-add x9 -> x0, other arithmetic: 33.5 us -> none  [the longest x4 16.1 us: batch_grads(): gradient = gradient.at[sources].add(grad_src).at[targets].add(grad_dst)]
    dot_general x12 -> x5, matrix products: 31.6 us -> 5.25 us  [the longest x1 2.43 us: local(): jnp.dot(wanted, embedding, precision=HI).reshape(owners, capacity, width)]
    all_to_all x0 -> x1, blocking collectives: none -> 11.1 us  [local(): lax.all_to_all(gradient.reshape(owners, capacity, width), 'dom', split_ax...]
    all_to_all x2 -> x1, starting transfers between devices: 9.63 us -> 3.41 us  [local(): lax.all_to_all(picked, 'dom', split_axis=0, concat_axis=0, tiled=True)]
    add x4 -> x1, local copies, waits for them, and re-layouts: 5.48 us -> 0.09 us  [slot_gradient(): return jnp.dot(mixed + mixed.T, buffer, precision=HI)]
    all_to_all x2 -> x1, waiting for transfers between devices: 12.1 us -> 7.25 us  [local(): lax.all_to_all(picked, 'dom', split_axis=0, concat_axis=0, tiled=True)]
    all_to_all x1, waiting for transfers between devices: 0.01 us -> 3.66 us  [local(): lax.all_to_all(requests, 'dom', split_axis=0, concat_axis=0, tiled=True)]
  transfers between devices with their start and end apart: 4 -> 3, of which waited for: 3 -> 3; matrix products, arithmetic and copies ran while one was open for 8% -> 4% of each run, Pallas kernels for 0% -> 0%
where the time goes in v1:
time: 94.4 us; the launch traced here: 93.9 us
  waiting for transfers between devices  44.6 us (47%)
  between operations  14.1 us (15%)
  blocking collectives  11.1 us (12%)
  starting transfers between devices  10.8 us (11%)
  other arithmetic  5.75 us (6%)
  matrix products  5.25 us (6%)
  local copies, waits for them, and re-layouts  2.25 us (2%)
    psum x1, waiting for transfers between devices, local(): summed = lax.psum(owned, 'rep')  33.7 us
    all_to_all x1, blocking collectives, local(): lax.all_to_all(gradient.reshape(owners, capacity, width), 'dom', split_ax...  11.1 us
    all_to_all x1, starting transfers between devices, local(): lax.all_to_all(requests, 'dom', split_axis=0, concat_axis=0, tiled=True)  7.32 us
    all_to_all x1, waiting for transfers between devices, local(): lax.all_to_all(picked, 'dom', split_axis=0, concat_axis=0, tiled=True)  7.25 us
    all_to_all x1, waiting for transfers between devices, local(): lax.all_to_all(requests, 'dom', split_axis=0, concat_axis=0, tiled=True)  3.66 us
    all_to_all x1, starting transfers between devices, local(): lax.all_to_all(picked, 'dom', split_axis=0, concat_axis=0, tiled=True)  3.41 us
    dot_general x1, matrix products, local(): jnp.dot(wanted, embedding, precision=HI).reshape(owners, capacity, width)  2.43 us
  transfers between devices with their start and end apart: 3, of which 3 were waited for; matrix products, arithmetic and copies ran while one was open for 4% of the time, Pallas kernels for 0%

profile of v1, /device:TPU:0, one launch (start us, length us, event | category | flops | bytes accessed | tf_op | source)
XLA Modules:
  0.0 93.9 jit_solution(3573747049158730609)
XLA Ops:
  7.2 7.3 %all-to-all-start = ((s32[8,1,16]{2,1,0:T(1,128)}), s32[8,1,16]{2,1,0:T(1,128)S(1)}, u32[]{:S(2)}, u32[]{:S(2)}) async-start(s32[8,1,16]{2,1,0:T(1,128)} %bitcast.37), calls=%async_computation | async-start | bytes 8192 | tf_op jit(solution)/shard_map/all_to_all | solution.py:43
  14.5 1.3 %convert_reduce_fusion = f32[2,2,512]{2,1,0:T(2,128)S(1)} fusion(s32[2,2,512]{2,1,0:T(2,128)} %bitcast.36), kind=kLoop, calls=%fused_computation | loop fusion | flops 3143680 | bytes 16384 | tf_op jit(solution)/shard_map/reduce_sum | solution.py:17
  15.8 0.7 copy.30
  16.5 0.0 copy-start.2
  16.5 0.8 copy.29
  17.2 3.7 %all-to-all-done = s32[8,1,16]{2,1,0:T(1,128)S(1)} async-done(((s32[8,1,16]{2,1,0:T(1,128)}), s32[8,1,16]{2,1,0:T(1,128)S(1)}, u32[]{:S(2)}, u32[]{:S(2)}) %all-to-all-start) | async-done | bytes 544 | tf_op jit(solution)/shard_map/all_to_all | solution.py:43
  20.9 0.5 broadcast.37
  21.4 0.0 copy-start.3
  21.4 0.7 reduce.3
  22.1 0.1 eq.78
  22.2 2.4 %fusion.4 = f32[128,400]{1,0:T(8,128)} fusion(f32[512,400]{0,1:T(8,128)} %param.6, s32[128]{0:T(128)S(1)} %eq.78), kind=kOutput, calls=%fused_computation.20 | convolution fusion | flops 314638336 | bytes 1024512 | tf_op jit(solution)/shard_map/dot_general | solution.py:45
  24.6 3.4 %all-to-all-start.1 = ((f32[8,16,400]{2,1,0:T(8,128)}), f32[8,16,400]{2,1,0:T(8,128)S(1)}, u32[]{:S(2)}, u32[]{:S(2)}) async-start(f32[8,16,400]{2,1,0:T(8,128)} %bitcast.5), calls=%async_computation.1 | async-start | bytes 524288 | tf_op jit(solution)/shard_map/all_to_all | solution.py:46
  28.0 0.0 all-reduce.2.cloned.1.call-start
  28.1 0.0 copy-done.2
  28.1 0.3 convert_reduce_fusion.2
  28.4 0.0 copy-done.3
  28.4 0.3 select_reduce_fusion.1
  28.8 0.1 add_reduce_fusion
  28.9 7.2 %all-to-all-done.1 = f32[8,16,400]{2,1,0:T(8,128)S(1)} async-done(((f32[8,16,400]{2,1,0:T(8,128)}), f32[8,16,400]{2,1,0:T(8,128)S(1)}, u32[]{:S(2)}, u32[]{:S(2)}) %all-to-all-start.1) | async-done | bytes 204832 | tf_op jit(solution)/shard_map/all_to_all | solution.py:46
  36.2 0.4 fusion.9
  36.6 0.6 fusion
  37.2 0.1 copy.21
  37.3 0.1 copy.22
  37.4 0.4 fusion.10
  37.8 11.1 %all_to_all.19 = f32[8,16,400]{2,1,0:T(8,128)S(1)} all-to-all(f32[8,16,400]{2,1,0:T(8,128)S(1)} %fusion.10), channel_id=1, replica_groups=mesh['dom'=8,'rep'=4] {'dom'}, dimensions={0} | all-to-all | bytes 409600 | tf_op jit(solution)/shard_map/all_to_all | solution.py:49
  48.9 1.5 %fusion.3 = f32[512,400]{0,1:T(8,128)} fusion(f32[128,400]{1,0:T(8,128)S(1)} %bitcast.30, s32[128]{0:T(128)S(1)} %eq.78), kind=kOutput, calls=%fused_computation.19 | convolution fusion | flops 314638336 | bytes 1024512 | tf_op jit(solution)/shard_map/dot_general | solution.py:52
  50.4 0.0 copy-start.4
  50.4 0.0 copy-start.1
  50.4 0.0 all-reduce.2.cloned.1.call-update
  50.4 33.7 %all-reduce.2.cloned.1.call-done = f32[512,400]{0,1:T(8,128)} async-done(((f32[512,400]{0,1:T(8,128)}), f32[512,400]{0,1:T(8,128)}) %all-reduce.2.cloned.1.call-update) | async-done | bytes 819216 | tf_op jit(solution)/shard_map/psum | solution.py:53
  84.1 0.0 copy-start
  84.1 1.3 %multiply_reduce_fusion = f32[512]{0:T(512)S(1)} fusion(f32[512,400]{0,1:T(8,128)} %all-reduce.2.cloned.1.call-done), kind=kLoop, calls=%fused_computation.5 | loop fusion | flops 409088 | bytes 821248 | tf_op jit(solution)/shard_map/reduce_sum | solution.py:34
  85.4 0.0 copy-done.4
  85.4 0.6 fusion.7
  86.0 0.0 copy-done.1
  86.0 0.0 copy-done
  86.0 1.1 %divide_subtract_fusion = f32[512,400]{0,1:T(8,128)} fusion(f32[512,400]{0,1:T(8,128)S(1)} %copy-done.1, f32[512,400]{0,1:T(8,128)S(1)} %copy-done, f32[512]{0:T(512)S(1)} %get-tuple-element.6), kind=kLoop, calls=%fused_computation.4 | loop fusion | flops 614400 | bytes 2459648 | tf_op jit(solution)/shard_map/sub | solution.py:35
  (3 shorter events, 0.0 us)
Async XLA Ops:
  7.2 13.7 %all-to-all-start = ((s32[8,1,16]{2,1,0:T(1,128)}), s32[8,1,16]{2,1,0:T(1,128)S(1)}, u32[]{:S(2)}, u32[]{:S(2)}) async-start(s32[8,1,16]{2,1,0:T(1,128)} %bitcast.37), calls=%async_computation | async-start | bytes 8192 | tf_op jit(solution)/shard_map/all_to_all | solution.py:43
  16.5 11.6 %copy-start.2 = (s32[1,1,2,512]{3,2,1,0:T(2,128)S(1)}, s32[1,1,2,512]{3,2,1,0:T(2,128)}, u32[]{:S(2)}) copy-start(s32[1,1,2,512]{3,2,1,0:T(2,128)} %param.9) | copy-start | bytes 12292
  21.4 7.0 %copy-start.3 = (s32[1,1,2,512]{3,2,1,0:T(2,128)S(1)}, s32[1,1,2,512]{3,2,1,0:T(2,128)}, u32[]{:S(2)}) copy-start(s32[1,1,2,512]{3,2,1,0:T(2,128)} %param.10) | copy-start | bytes 12292
  24.6 11.6 %all-to-all-start.1 = ((f32[8,16,400]{2,1,0:T(8,128)}), f32[8,16,400]{2,1,0:T(8,128)S(1)}, u32[]{:S(2)}, u32[]{:S(2)}) async-start(f32[8,16,400]{2,1,0:T(8,128)} %bitcast.5), calls=%async_computation.1 | async-start | bytes 524288 | tf_op jit(solution)/shard_map/all_to_all | solution.py:46
  28.0 56.1 %all-reduce.2.cloned.1.call-start = ((), (), s32[]{:S(2)}) async-start(), calls=%async_computation.3 | async-start | bytes 1638400 | tf_op jit(solution)/shard_map/psum | solution.py:53
  50.4 35.0 %copy-start.4 = (f32[512]{0:T(512)S(1)}, f32[512]{0:T(512)}, u32[]{:S(2)}) copy-start(f32[512]{0:T(512)} %param.7) | copy-start | bytes 6148
  50.4 35.6 %copy-start.1 = (f32[512,400]{0,1:T(8,128)S(1)}, f32[512,400]{0,1:T(8,128)}, u32[]{:S(2)}) copy-start(f32[512,400]{0,1:T(8,128)} %param.6) | copy-start | bytes 2457604
  84.1 1.9 %copy-start = (f32[512,400]{0,1:T(8,128)S(1)}, f32[512,400]{0,1:T(8,128)}, u32[]{:S(2)}) copy-start(f32[512,400]{0,1:T(8,128)} %all-reduce.2.cloned.1.call-done) | copy-start | bytes 2457604
Sparse Core Ops, SparseCore 0:
  50.5 33.5 all-reduce.1

commit v2 on v1

v2 whole, which is shorter than its diff:
```python
import functools
import jax
import jax.numpy as jnp
from jax import lax
from jax.experimental import pallas as pl
from jax.experimental.pallas import tpu as pltpu
from jax.sharding import PartitionSpec as P

learn_rate = 0.1
HI = lax.Precision.HIGHEST
HEAVY = 4
LIGHT_ROWS = 8
MESH = pl.DeviceIdType.MESH
BF = jnp.bfloat16
F32 = jnp.float32


def mm(a, b):
    return lax.dot_general(a, b, (((1,), (0,)), ((), ())), preferred_element_type=F32)


def mm_nt(a, b):
    return lax.dot_general(a, b, (((1,), (1,)), ((), ())), preferred_element_type=F32)


def parts_of(x, count):
    parts = []
    for _ in range(count):
        part = x.astype(BF)
        parts.append(part)
        x = x - part.astype(F32)
    return parts


def hot(mask):
    return mask.astype(F32).astype(BF)


def pair_counts(src_ref, dst_ref, neg_ref, slots):
    batches, edges = src_ref.shape[2:]
    samples = neg_ref.shape[4]
    slot_id = lax.broadcasted_iota(jnp.int32, (slots, edges), 0)
    edge_id = lax.broadcasted_iota(jnp.int32, (edges, samples), 0)
    ones = jnp.ones((8, samples), BF)
    pairs = jnp.zeros((slots, slots), F32)
    counts = jnp.zeros((slots, slots), F32)
    for b in range(batches):
        src_mask = (slot_id == src_ref[0, 0, b : b + 1, :]).astype(F32)
        dst_mask = (slot_id == dst_ref[0, 0, b : b + 1, :]).astype(F32)
        src_hot = src_mask.astype(BF)
        dst_hot = dst_mask.astype(BF)
        counts += mm_nt(src_hot, dst_hot)
        for side, (near, far) in enumerate(((src_mask, dst_hot), (dst_mask, src_hot))):
            chosen = hot(edge_id == neg_ref[0, 0, b, side : side + 1, :])
            negative = mm(far, chosen).astype(BF)
            times = mm_nt(ones, negative)[0:1, :]
            pairs += jnp.sum(near, axis=1, keepdims=True) * times
    return (pairs + pairs.T) * (1.0 / samples), counts + counts.T


def kernel(
    ndom, nrep,
    emb_ref, lists_ref, src_ref, dst_ref, neg_ref, out_ref,
    req_send, req_recv, pull_send, buf, grad_send, grad_recv, ids_all,
    req_ss, req_rs, pull_ss, pull_rs, ret_ss, ret_rs, rep_ss, rep_rs, ids_ss, ids_rs,
):
    me = lax.axis_index("dom")
    rep = lax.axis_index("rep")
    rows, width = emb_ref.shape
    capacity = lists_ref.shape[3]
    slots = ndom * capacity

    def up(c):
        return lax.rem(me + c, ndom)

    def down(c):
        return lax.rem(me + ndom - c, ndom)

    def rep_peer(k):
        return lax.rem(rep + k, nrep)

    def size(c):
        return capacity if c < HEAVY else min(LIGHT_ROWS, capacity)

    buf[...] = jnp.zeros_like(buf)
    grad_recv[...] = jnp.zeros_like(grad_recv)
    own_lists = lists_ref[0, 0]
    if slots > capacity:
        own_lists = jnp.concatenate([own_lists, jnp.zeros((ndom, slots - capacity), jnp.int32)], axis=1)
    own_lists = pltpu.roll(own_lists, me * capacity, 1)
    for o in range(ndom):
        req_send[o] = jnp.broadcast_to(own_lists[o : o + 1, :], (8, slots))

    barrier = pltpu.get_barrier_semaphore()
    for c in range(1, ndom):
        pl.semaphore_signal(barrier, inc=1, device_id={"dom": up(c)}, device_id_type=MESH)
    for k in range(1, nrep):
        pl.semaphore_signal(barrier, inc=1, device_id={"rep": rep_peer(k)}, device_id_type=MESH)
    pl.semaphore_wait(barrier, ndom - 1 + nrep - 1)

    def remote(src, dst, send, recv, target):
        return pltpu.make_async_remote_copy(
            src_ref=src, dst_ref=dst, send_sem=send, recv_sem=recv, device_id=target, device_id_type=MESH
        )

    asks = []
    for c in range(1, ndom):
        ask = remote(req_send.at[up(c)], req_recv.at[c], req_ss.at[c], req_rs.at[c], {"dom": up(c)})
        ask.start()
        asks.append(ask)

    pairs, counts = pair_counts(src_ref, dst_ref, neg_ref, slots)
    emb_parts = parts_of(emb_ref[...], 3)

    ids = req_send[me]
    for c in range(1, ndom):
        asks[c - 1].wait_recv()
        ids = ids + req_recv[c]
    ids_all[rep] = ids

    wanted = hot(lax.broadcasted_iota(jnp.int32, (slots, rows), 1) == ids.T[:, 0:1])
    pulled = mm(wanted, emb_parts[0]) + mm(wanted, emb_parts[1]) + mm(wanted, emb_parts[2])
    pull_send[...] = pulled.reshape(ndom, capacity, width)
    pulls = []
    for c in range(1, ndom):
        live = pl.ds(0, size(c))
        pull = remote(
            pull_send.at[down(c), live], buf.at[me, live], pull_ss.at[c], pull_rs.at[c], {"dom": down(c)}
        )
        pull.start()
        pulls.append(pull)
    buf[me] = pull_send[me]
    tells = []
    for k in range(1, nrep):
        tell = remote(ids_all.at[rep], ids_all.at[rep], ids_ss.at[k], ids_rs.at[k], {"rep": rep_peer(k)})
        tell.start()
        tells.append(tell)

    for c in range(1, ndom):
        live = pl.ds(0, size(c))
        remote(buf.at[up(c), live], buf.at[up(c), live], pull_ss.at[c], pull_rs.at[c], {"dom": up(c)}).wait_recv()
    buffer = buf[...].reshape(slots, width)
    gram = lax.dot_general(buffer, buffer, (((1,), (1,)), ((), ())), precision=HI, preferred_element_type=F32)
    mixed = pairs * jax.nn.sigmoid(gram) - counts * jax.nn.sigmoid(-gram)
    gradient = jnp.dot(mixed, buffer, precision=HI, preferred_element_type=F32)
    grad_send[...] = gradient.reshape(ndom, capacity, width)

    returns = []
    for c in range(1, ndom):
        live = pl.ds(0, size(c))
        back = remote(
            grad_send.at[up(c), live], grad_recv.at[rep, me, live], ret_ss.at[c], ret_rs.at[c], {"dom": up(c)}
        )
        back.start()
        returns.append(back)
    grad_recv[rep, me] = grad_send[me]

    shares = []
    for c in range(ndom):
        block = grad_recv.at[rep, down(c), pl.ds(0, size(c))]
        if c > 0:
            remote(block, block, ret_ss.at[c], ret_rs.at[c], {"dom": down(c)}).wait_recv()
        for k in range(1, nrep):
            share = remote(block, block, rep_ss.at[k, c], rep_rs.at[k, c], {"rep": rep_peer(k)})
            share.start()
            shares.append(share)

    for k in range(1, nrep):
        tells[k - 1].wait_recv()
        source = rep_peer(nrep - k)
        for c in range(ndom):
            block = grad_recv.at[source, down(c), pl.ds(0, size(c))]
            remote(block, block, rep_ss.at[k, c], rep_rs.at[k, c], {"rep": source}).wait_recv()

    row_id = lax.broadcasted_iota(jnp.int32, (rows, slots), 0)
    total = jnp.zeros((rows, width), F32)
    for g in range(nrep):
        owned = hot(row_id == ids_all[g, 0:1, :])
        for part in parts_of(grad_recv[g].reshape(slots, width), 2):
            total += mm(owned, part)
    out_ref[...] = total

    for copy in asks + pulls + tells + returns + shares:
        copy.wait_send()


def local(ndom, nrep, embedding, adagrad_sum, row_lists, source_slots, target_slots, negative_ids):
    rows, width = embedding.shape
    capacity = row_lists.shape[3]
    slots = ndom * capacity
    dma = pltpu.SemaphoreType.DMA
    vmem = pl.BlockSpec(memory_space=pltpu.VMEM)
    row_grad = pl.pallas_call(
        functools.partial(kernel, ndom, nrep),
        out_shape=jax.ShapeDtypeStruct((rows, width), F32),
        in_specs=[vmem] * 5,
        out_specs=vmem,
        scratch_shapes=[
            pltpu.VMEM((ndom, 8, slots), jnp.int32),
            pltpu.VMEM((ndom, 8, slots), jnp.int32),
            pltpu.VMEM((ndom, capacity, width), F32),
            pltpu.VMEM((ndom, capacity, width), F32),
            pltpu.VMEM((ndom, capacity, width), F32),
            pltpu.VMEM((nrep, ndom, capacity, width), F32),
            pltpu.VMEM((nrep, 8, slots), jnp.int32),
            dma((ndom,)), dma((ndom,)), dma((ndom,)), dma((ndom,)), dma((ndom,)), dma((ndom,)),
            dma((nrep, ndom)), dma((nrep, ndom)), dma((nrep,)), dma((nrep,)),
        ],
        compiler_params=pltpu.CompilerParams(
            collective_id=0, has_side_effects=True, vmem_limit_bytes=60 * 1024 * 1024
        ),
    )(embedding, row_lists, source_slots, target_slots, negative_ids)
    new_sum = adagrad_sum + jnp.mean(row_grad * row_grad, axis=1)
    new_rows = embedding - learn_rate * row_grad / jnp.sqrt(new_sum)[:, None]
    return (new_rows, new_sum)


def solution(mesh):
    in_specs = (
        P("dom", None),
        P("dom"),
        P("rep", "dom", None, None),
        P("rep", "dom", None, None),
        P("rep", "dom", None, None),
        P("rep", "dom", None, None, None),
    )
    out_specs = (P("dom", None), P("dom"))
    body = functools.partial(local, mesh.shape["dom"], mesh.shape["rep"])
    return jax.shard_map(body, mesh=mesh, in_specs=in_specs, out_specs=out_specs, check_vma=False)
```

time: 94.4 us -> 39.2 us (0.42)
  the two profiles are of different devices: /device:TPU:0 before, /device:TPU:1 now
where the time goes in v2:
time: 39.2 us; the launch traced here: 38.6 us
  Pallas kernels  30.7 us (78%)
  local copies, waits for them, and re-layouts  3.68 us (9%)
  other arithmetic  3.5 us (9%)
  between operations  0.67 us (2%)
    pallas_call x1, Pallas kernels, local(): pl.pallas_call(functools.partial(kernel, ndom, nrep), out_shape=jax.Shape...  30.7 us
    unnamed x6, local copies, waits for them, and re-layouts  3.68 us
    reduce_sum x1, other arithmetic, local(): new_sum = adagrad_sum + jnp.mean(row_grad * row_grad, axis=1)  1.47 us
    sub x1, other arithmetic, local(): new_rows = embedding - learn_rate * row_grad / jnp.sqrt(new_sum)[:, None]  1.45 us

profile of v2, /device:TPU:1, one launch (start us, length us, event | category | flops | bytes accessed | tf_op | source)
XLA Modules:
  0.0 38.6 jit_solution(2000419668644865779)
XLA Ops:
  0.6 2.5 %copy.9.emb_ref = f32[512,400]{1,0:T(8,128)} copy(f32[512,400]{0,1:T(8,128)} %param.6) | data formatting | bytes 1638400 | tf_op args[0]
  3.1 30.7 %shard_map.77 = f32[512,400]{1,0:T(8,128)} custom-call(f32[512,400]{1,0:T(8,128)} %copy.9.emb_ref, s32[1,1,8,16]{3,2,1,0:T(8,128)} %lists_ref.1, s32[1,1,2,512]{3,2,1,0:T(2,128)} %src_ref.1, s32[1,1,2,512]{3,2,1,0:T(2,128)} %dst_ref.1, s32[1,1,2,2,512]{4,3,2,1,0:T(2,128)} %neg_ref.1), custom_call_target="tpu_custom_call" | custom-call | tf_op jit(solution)/shard_map/pallas_call | solution.py:193
  33.8 0.0 copy-start.1
  33.9 0.0 copy-start
  33.9 1.5 %multiply_reduce_fusion = f32[512]{0:T(512)S(1)} fusion(f32[512,400]{1,0:T(8,128)} %shard_map.77), kind=kLoop, calls=%fused_computation.1 | loop fusion | flops 409088 | bytes 821248 | tf_op jit(solution)/shard_map/reduce_sum | solution.py:213
  35.3 0.0 copy-done.1
  35.3 0.6 %fusion = (f32[512]{0:T(512)S(1)}, f32[512]{0:T(512)}) fusion(f32[512]{0:T(512)S(1)} %copy-done.1, f32[512]{0:T(512)S(1)} %multiply_reduce_fusion), kind=kLoop, calls=%fused_computation.3 | loop fusion | flops 1024 | bytes 8192 | tf_op jit(solution)/shard_map/sqrt | solution.py:214
  35.9 0.0 copy-done
  35.9 1.4 %divide_subtract_fusion = f32[512,400]{1,0:T(8,128)S(1)} fusion(f32[512,400]{1,0:T(8,128)S(1)} %copy-done, f32[512,400]{1,0:T(8,128)} %shard_map.77, f32[512]{0:T(512)S(1)} %get-tuple-element.4), kind=kLoop, calls=%fused_computation | loop fusion | flops 614400 | bytes 2459648 | tf_op jit(solution)/shard_map/sub | solution.py:214
  37.4 1.2 %copy.10 = f32[512,400]{0,1:T(8,128)} copy(f32[512,400]{1,0:T(8,128)S(1)} %divide_subtract_fusion) | data formatting | bytes 1638400
Async XLA Ops:
  33.8 1.5 %copy-start.1 = (f32[512]{0:T(512)S(1)}, f32[512]{0:T(512)}, u32[]{:S(2)}) copy-start(f32[512]{0:T(512)} %param.7) | copy-start | bytes 6148
  33.9 2.1 %copy-start = (f32[512,400]{1,0:T(8,128)S(1)}, f32[512,400]{1,0:T(8,128)}, u32[]{:S(2)}) copy-start(f32[512,400]{1,0:T(8,128)} %copy.9.emb_ref) | copy-start | bytes 2457604

commit v3 on v2

--- a/solution.py
+++ b/solution.py
@@ -60,15 +60,17 @@
 
 def kernel(
     ndom, nrep,
-    emb_ref, lists_ref, src_ref, dst_ref, neg_ref, out_ref,
-    req_send, req_recv, pull_send, buf, grad_send, grad_recv, ids_all,
-    req_ss, req_rs, pull_ss, pull_rs, ret_ss, ret_rs, rep_ss, rep_rs, ids_ss, ids_rs,
+    emb_hbm, sum_hbm, lists_hbm, src_hbm, dst_hbm, neg_hbm, rows_out, sum_out,
+    emb_ref, sum_ref, lists_ref, src_ref, dst_ref, neg_ref,
+    req_send, req_recv, pull_send, buf, grad_send, grad_recv, ids_all, halves,
+    in_sem, req_ss, req_rs, pull_ss, pull_rs, ret_ss, ret_rs, rep_ss, rep_rs, ids_ss, ids_rs,
 ):
     me = lax.axis_index("dom")
     rep = lax.axis_index("rep")
-    rows, width = emb_ref.shape
+    width, rows = emb_ref.shape
     capacity = lists_ref.shape[3]
     slots = ndom * capacity
+    relay = nrep == 4
 
     def up(c):
         return lax.rem(me + c, ndom)
@@ -77,25 +79,46 @@
         return lax.rem(me + ndom - c, ndom)
 
     def rep_peer(k):
-        return lax.rem(rep + k, nrep)
+        flipped = rep
+        bit = 1
+        while bit < nrep:
+            if k & bit:
+                flipped = flipped + bit - 2 * bit * lax.rem(rep // bit, 2)
+            bit *= 2
+        return flipped
 
     def size(c):
         return capacity if c < HEAVY else min(LIGHT_ROWS, capacity)
 
-    buf[...] = jnp.zeros_like(buf)
-    grad_recv[...] = jnp.zeros_like(grad_recv)
+    barrier = pltpu.get_barrier_semaphore()
+    for c in range(1, ndom):
+        pl.semaphore_signal(barrier, inc=1, device_id={"dom": up(c)}, device_id_type=MESH)
+    for k in range(1, nrep):
+        pl.semaphore_signal(barrier, inc=1, device_id={"rep": rep_peer(k)}, device_id_type=MESH)
+
+    loads = []
+    for i, (hbm, ref) in enumerate((
+        (lists_hbm, lists_ref), (src_hbm, src_ref), (dst_hbm, dst_ref), (neg_hbm, neg_ref), (emb_hbm, emb_ref), (sum_hbm, sum_ref)
+    )):
+        load = pltpu.make_async_copy(hbm, ref, in_sem.at[i])
+        load.start()
+        loads.append(load)
+
+    for c in range(ndom):
+        if size(c) < capacity:
+            rest = capacity - size(c)
+            buf[up(c), size(c) :, :] = jnp.zeros((rest, width), F32)
+            for g in range(nrep):
+                grad_recv[g, down(c), size(c) :, :] = jnp.zeros((rest, width), F32)
+
+    loads[0].wait()
     own_lists = lists_ref[0, 0]
     if slots > capacity:
         own_lists = jnp.concatenate([own_lists, jnp.zeros((ndom, slots - capacity), jnp.int32)], axis=1)
     own_lists = pltpu.roll(own_lists, me * capacity, 1)
     for o in range(ndom):
-        req_send[o] = jnp.broadcast_to(own_lists[o : o + 1, :], (8, slots))
-
-    barrier = pltpu.get_barrier_semaphore()
-    for c in range(1, ndom):
-        pl.semaphore_signal(barrier, inc=1, device_id={"dom": up(c)}, device_id_type=MESH)
-    for k in range(1, nrep):
-        pl.semaphore_signal(barrier, inc=1, device_id={"rep": rep_peer(k)}, device_id_type=MESH)
+        req_send[o] = own_lists[o : o + 1, :]
+
     pl.semaphore_wait(barrier, ndom - 1 + nrep - 1)
 
     def remote(src, dst, send, recv, target):
@@ -109,8 +132,10 @@
         ask.start()
         asks.append(ask)
 
+    for load in loads[1:]:
+        load.wait()
+    emb_parts = parts_of(emb_ref[...], 3)
     pairs, counts = pair_counts(src_ref, dst_ref, neg_ref, slots)
-    emb_parts = parts_of(emb_ref[...], 3)
 
     ids = req_send[me]
     for c in range(1, ndom):
@@ -118,8 +143,13 @@
         ids = ids + req_recv[c]
     ids_all[rep] = ids
 
-    wanted = hot(lax.broadcasted_iota(jnp.int32, (slots, rows), 1) == ids.T[:, 0:1])
-    pulled = mm(wanted, emb_parts[0]) + mm(wanted, emb_parts[1]) + mm(wanted, emb_parts[2])
+    row_id = lax.broadcasted_iota(jnp.int32, (slots, rows), 1)
+
+    def hot_rows(row):
+        return hot(row_id == jnp.broadcast_to(row, (8, slots)).T[:, 0:1])
+
+    wanted = hot_rows(ids)
+    pulled = mm_nt(wanted, emb_parts[0]) + mm_nt(wanted, emb_parts[1]) + mm_nt(wanted, emb_parts[2])
     pull_send[...] = pulled.reshape(ndom, capacity, width)
     pulls = []
     for c in range(1, ndom):
@@ -137,8 +167,8 @@
         tells.append(tell)
 
     for c in range(1, ndom):
-        live = pl.ds(0, size(c))
-        remote(buf.at[up(c), live], buf.at[up(c), live], pull_ss.at[c], pull_rs.at[c], {"dom": up(c)}).wait_recv()
+        block = buf.at[up(c), pl.ds(0, size(c))]
+        remote(block, block, pull_ss.at[c], pull_rs.at[c], {"dom": up(c)}).wait_recv()
     buffer = buf[...].reshape(slots, width)
     gram = lax.dot_general(buffer, buffer, (((1,), (1,)), ((), ())), precision=HI, preferred_element_type=F32)
     mixed = pairs * jax.nn.sigmoid(gram) - counts * jax.nn.sigmoid(-gram)
@@ -155,30 +185,61 @@
         returns.append(back)
     grad_recv[rep, me] = grad_send[me]
 
+    direct = [2, 1] if relay else list(range(1, nrep))
+
+    def share(g, c, k, to):
+        block = grad_recv.at[g, down(c), pl.ds(0, size(c))]
+        return remote(block, block, rep_ss.at[k, c], rep_rs.at[k, c], {"rep": to})
+
     shares = []
     for c in range(ndom):
-        block = grad_recv.at[rep, down(c), pl.ds(0, size(c))]
         if c > 0:
+            block = grad_recv.at[rep, down(c), pl.ds(0, size(c))]
             remote(block, block, ret_ss.at[c], ret_rs.at[c], {"dom": down(c)}).wait_recv()
-        for k in range(1, nrep):
-            share = remote(block, block, rep_ss.at[k, c], rep_rs.at[k, c], {"rep": rep_peer(k)})
-            share.start()
-            shares.append(share)
-
-    for k in range(1, nrep):
-        tells[k - 1].wait_recv()
-        source = rep_peer(nrep - k)
+        for k in direct:
+            sent = share(rep, c, k, rep_peer(k))
+            sent.start()
+            shares.append(sent)
+
+    for tell in tells:
+        tell.wait_recv()
+
+    def arrived(k, c):
+        share(rep_peer(k), c, k, rep_peer(k)).wait_recv()
+
+    def half_sum(half, first):
+        groups = max(nrep // 2, 1)
+        total = jnp.zeros((width, rows), F32)
+        hots = [hot_rows(ids_all[first + g]) for g in range(groups)]
+        stacked = jnp.concatenate(hots, axis=0)
+        data = grad_recv[pl.ds(first, groups)].reshape(groups * slots, width)
+        for part in parts_of(data, 2):
+            total += lax.dot_general(part, stacked, (((0,), (0,)), ((), ())), preferred_element_type=F32)
+        halves[half] = total
+
+    if relay:
+        chip = rep // 2
         for c in range(ndom):
-            block = grad_recv.at[source, down(c), pl.ds(0, size(c))]
-            remote(block, block, rep_ss.at[k, c], rep_rs.at[k, c], {"rep": source}).wait_recv()
-
-    row_id = lax.broadcasted_iota(jnp.int32, (rows, slots), 0)
-    total = jnp.zeros((rows, width), F32)
-    for g in range(nrep):
-        owned = hot(row_id == ids_all[g, 0:1, :])
-        for part in parts_of(grad_recv[g].reshape(slots, width), 2):
-            total += mm(owned, part)
-    out_ref[...] = total
+            arrived(1, c)
+        half_sum(chip, 2 * chip)
+        for c in range(ndom):
+            arrived(2, c)
+            sent = share(rep_peer(2), c, 3, rep_peer(1))
+            sent.start()
+            shares.append(sent)
+        for c in range(ndom):
+            arrived(3, c)
+        half_sum(1 - chip, 2 - 2 * chip)
+    else:
+        for k in direct:
+            for c in range(ndom):
+                arrived(k, c)
+        half_sum(0, 0)
+        half_sum(1, nrep // 2)
+    row_grad = halves[0] + halves[1]
+    new_sum = sum_ref[...] + jnp.sum(row_grad * row_grad, axis=0, keepdims=True) * (1.0 / width)
+    sum_out[...] = new_sum
+    rows_out[...] = emb_ref[...] - row_grad * (learn_rate / jnp.sqrt(new_sum))
 
     for copy in asks + pulls + tells + returns + shares:
         copy.wait_send()
@@ -190,29 +251,35 @@
     slots = ndom * capacity
     dma = pltpu.SemaphoreType.DMA
     vmem = pl.BlockSpec(memory_space=pltpu.VMEM)
-    row_grad = pl.pallas_call(
+    new_rows, new_sum = pl.pallas_call(
         functools.partial(kernel, ndom, nrep),
-        out_shape=jax.ShapeDtypeStruct((rows, width), F32),
-        in_specs=[vmem] * 5,
-        out_specs=vmem,
+        out_shape=(jax.ShapeDtypeStruct((width, rows), F32), jax.ShapeDtypeStruct((1, rows), F32)),
+        in_specs=[pl.BlockSpec(memory_space=pl.ANY)] * 6,
+        out_specs=(vmem, vmem),
         scratch_shapes=[
-            pltpu.VMEM((ndom, 8, slots), jnp.int32),
-            pltpu.VMEM((ndom, 8, slots), jnp.int32),
+            pltpu.VMEM((width, rows), F32),
+            pltpu.VMEM((1, rows), F32),
+            pltpu.VMEM(row_lists.shape, jnp.int32),
+            pltpu.VMEM(source_slots.shape, jnp.int32),
+            pltpu.VMEM(target_slots.shape, jnp.int32),
+            pltpu.VMEM(negative_ids.shape, jnp.int32),
+            pltpu.VMEM((ndom, 1, slots), jnp.int32),
+            pltpu.VMEM((ndom, 1, slots), jnp.int32),
             pltpu.VMEM((ndom, capacity, width), F32),
             pltpu.VMEM((ndom, capacity, width), F32),
             pltpu.VMEM((ndom, capacity, width), F32),
             pltpu.VMEM((nrep, ndom, capacity, width), F32),
-            pltpu.VMEM((nrep, 8, slots), jnp.int32),
+            pltpu.VMEM((nrep, 1, slots), jnp.int32),
+            pltpu.VMEM((2, width, rows), F32),
+            dma((6,)),
             dma((ndom,)), dma((ndom,)), dma((ndom,)), dma((ndom,)), dma((ndom,)), dma((ndom,)),
             dma((nrep, ndom)), dma((nrep, ndom)), dma((nrep,)), dma((nrep,)),
         ],
         compiler_params=pltpu.CompilerParams(
             collective_id=0, has_side_effects=True, vmem_limit_bytes=60 * 1024 * 1024
         ),
-    )(embedding, row_lists, source_slots, target_slots, negative_ids)
-    new_sum = adagrad_sum + jnp.mean(row_grad * row_grad, axis=1)
-    new_rows = embedding - learn_rate * row_grad / jnp.sqrt(new_sum)[:, None]
-    return (new_rows, new_sum)
+    )(embedding.T, adagrad_sum.reshape(1, rows), row_lists, source_slots, target_slots, negative_ids)
+    return (new_rows.T, new_sum.reshape(rows))
 
 
 def solution(mesh):

time: 39.2 us -> 31.9 us (0.81); the launches traced: 38.6 us -> 31.8 us
  other arithmetic: 3.5 us -> 0 us
  Pallas kernels: 30.7 us -> 28.5 us
  local copies, waits for them, and re-layouts: 3.68 us -> 2.67 us
    pallas_call x1, Pallas kernels: 30.7 us -> 28.5 us  [local(): pl.pallas_call(functools.partial(kernel, ndom, nrep), out_shape=(jax.Shap...]
    reduce_sum x1 -> x0, other arithmetic: 1.47 us -> none  [local(): new_sum = adagrad_sum + jnp.mean(row_grad * row_grad, axis=1)]
    sub x1 -> x0, other arithmetic: 1.45 us -> none  [local(): new_rows = embedding - learn_rate * row_grad / jnp.sqrt(new_sum)[:, None]]
    unnamed x6 -> x4, local copies, waits for them, and re-layouts: 3.68 us -> 2.67 us
    sqrt x1 -> x0, other arithmetic: 0.58 us -> none  [local(): new_rows = embedding - learn_rate * row_grad / jnp.sqrt(new_sum)[:, None]]
where the time goes in v3:
time: 31.9 us; the launch traced here: 31.8 us
  Pallas kernels  28.5 us (89%)
  local copies, waits for them, and re-layouts  2.67 us (8%)
  between operations  0.65 us (2%)
    pallas_call x1, Pallas kernels, local(): pl.pallas_call(functools.partial(kernel, ndom, nrep), out_shape=(jax.Shap...  28.5 us
    unnamed x4, local copies, waits for them, and re-layouts  2.67 us

profile of v3, /device:TPU:1, one launch (start us, length us, event | category | flops | bytes accessed | tf_op | source)
XLA Modules:
  0.0 31.8 jit_solution(17048438507641904077)
XLA Ops:
  0.6 28.5 %shard_map.77 = (f32[400,512]{1,0:T(8,128)}, f32[1,512]{1,0:T(1,128)}) custom-call(f32[400,512]{1,0:T(8,128)} %bitcast.4, f32[1,512]{1,0:T(1,128)} %bitcast.6, s32[1,1,8,16]{3,2,1,0:T(8,128)} %lists_hbm.1, s32[1,1,2,512]{3,2,1,0:T(2,128)} %src_hbm.1, s32[1,1,2,512]{3,2,1,0:T(2,128)} %dst_hbm.1, s32[1,1,2,2,512]{4,3,2,1,0:T(2,128)} %neg_hbm.1), custom_call_target="tpu_custom_call" | custom-call | tf_op jit(solution)/shard_map/pallas_call | solution.py:254
  29.1 0.0 copy-start
  29.1 2.1 %copy.10 = f32[512,400]{0,1:T(8,128)} copy(f32[512,400]{0,1:T(8,128)} %bitcast.5) | data formatting | bytes 1638400
  31.2 0.0 copy-done
  31.2 0.6 %copy.11 = f32[512]{0:T(512)} copy(f32[512]{0:T(512)S(1)} %bitcast.7) | data formatting | bytes 4096
Async XLA Ops:
  29.1 2.1 %copy-start = (f32[1,512]{1,0:T(1,128)S(1)}, f32[1,512]{1,0:T(1,128)}, u32[]{:S(2)}) copy-start(f32[1,512]{1,0:T(1,128)} %get-tuple-element.5) | copy-start | bytes 6148

commit v4 on v3

v4 whole, which is shorter than its diff:
```python
import functools
import jax
import jax.numpy as jnp
from jax import lax
from jax.experimental import pallas as pl
from jax.experimental.pallas import tpu as pltpu
from jax.sharding import PartitionSpec as P

learn_rate = 0.1
HI = lax.Precision.HIGHEST
HEAVY = 4
LIGHT_ROWS = 8
MESH = pl.DeviceIdType.MESH
BF = jnp.bfloat16
F32 = jnp.float32


def mm(a, b):
    return lax.dot_general(a, b, (((1,), (0,)), ((), ())), preferred_element_type=F32)


def mm_nt(a, b):
    return lax.dot_general(a, b, (((1,), (1,)), ((), ())), preferred_element_type=F32)


def parts_of(x, count):
    parts = []
    for _ in range(count):
        part = x.astype(BF)
        parts.append(part)
        x = x - part.astype(F32)
    return parts


def hot(mask):
    return mask.astype(F32).astype(BF)


def pair_counts(src_ref, dst_ref, neg_ref, slots):
    batches, edges = src_ref.shape[2:]
    samples = neg_ref.shape[4]
    slot_id = lax.broadcasted_iota(jnp.int32, (slots, edges), 0)
    edge_id = lax.broadcasted_iota(jnp.int32, (edges, samples), 0)
    ones = jnp.ones((8, samples), BF)
    pairs = jnp.zeros((slots, slots), F32)
    counts = jnp.zeros((slots, slots), F32)
    for b in range(batches):
        src_mask = (slot_id == src_ref[0, 0, b : b + 1, :]).astype(F32)
        dst_mask = (slot_id == dst_ref[0, 0, b : b + 1, :]).astype(F32)
        src_hot = src_mask.astype(BF)
        dst_hot = dst_mask.astype(BF)
        counts += mm_nt(src_hot, dst_hot)
        for side, (near, far) in enumerate(((src_mask, dst_hot), (dst_mask, src_hot))):
            chosen = hot(edge_id == neg_ref[0, 0, b, side : side + 1, :])
            negative = mm(far, chosen).astype(BF)
            times = mm_nt(ones, negative)[0:1, :]
            pairs += jnp.sum(near, axis=1, keepdims=True) * times
    return (pairs + pairs.T) * (1.0 / samples), counts + counts.T


def kernel(
    ndom, nrep,
    emb_hbm, lists_hbm, src_hbm, dst_hbm, neg_hbm, total_out,
    emb_ref, lists_ref, src_ref, dst_ref, neg_ref,
    req_send, req_recv, pull_send, buf, grad_send, grad_recv, ids_all, halves,
    in_sem, req_ss, req_rs, pull_ss, pull_rs, ret_ss, ret_rs, rep_ss, rep_rs, ids_ss, ids_rs,
):
    me = lax.axis_index("dom")
    rep = lax.axis_index("rep")
    width, rows = emb_ref.shape
    capacity = lists_ref.shape[3]
    slots = ndom * capacity
    relay = nrep == 4

    def flip(index, count, k):
        flipped = index
        bit = 1
        while bit < count:
            if k & bit:
                flipped = flipped + bit - 2 * bit * lax.rem(index // bit, 2)
            bit *= 2
        return flipped

    paired = ndom & (ndom - 1) == 0

    def to(k):
        return flip(me, ndom, k) if paired else lax.rem(me + k, ndom)

    def source(k):
        return flip(me, ndom, k) if paired else lax.rem(me + ndom - k, ndom)

    def rep_peer(k):
        return flip(rep, nrep, k)

    light = min(LIGHT_ROWS, capacity)

    def units(owner, worker, act):
        act(0, pl.ds(0, light))
        if light < capacity:
            @pl.when(lax.rem(owner - worker + ndom, ndom) < HEAVY)
            def _():
                act(1, pl.ds(light, capacity - light))

    barrier = pltpu.get_barrier_semaphore()
    for c in range(1, ndom):
        pl.semaphore_signal(barrier, inc=1, device_id={"dom": to(c)}, device_id_type=MESH)
    for k in range(1, nrep):
        pl.semaphore_signal(barrier, inc=1, device_id={"rep": rep_peer(k)}, device_id_type=MESH)

    loads = []
    for i, (hbm, ref) in enumerate((
        (lists_hbm, lists_ref), (src_hbm, src_ref), (dst_hbm, dst_ref), (neg_hbm, neg_ref), (emb_hbm, emb_ref)
    )):
        load = pltpu.make_async_copy(hbm, ref, in_sem.at[i])
        load.start()
        loads.append(load)

    if light < capacity:
        for k in range(1, ndom):
            buf[source(k), light:, :] = jnp.zeros((capacity - light, width), F32)
            for g in range(nrep):
                @pl.when(lax.rem(me - source(k) + ndom, ndom) >= HEAVY)
                def _():
                    grad_recv[g, source(k), light:, :] = jnp.zeros((capacity - light, width), F32)

    loads[0].wait()
    own_lists = lists_ref[0, 0]
    if slots > capacity:
        own_lists = jnp.concatenate([own_lists, jnp.zeros((ndom, slots - capacity), jnp.int32)], axis=1)
    own_lists = pltpu.roll(own_lists, me * capacity, 1)
    for o in range(ndom):
        req_send[o] = own_lists[o : o + 1, :]

    pl.semaphore_wait(barrier, ndom - 1 + nrep - 1)

    def remote(src, dst, send, recv, target):
        return pltpu.make_async_remote_copy(
            src_ref=src, dst_ref=dst, send_sem=send, recv_sem=recv, device_id=target, device_id_type=MESH
        )

    asks = []
    for c in range(1, ndom):
        ask = remote(req_send.at[to(c)], req_recv.at[c], req_ss.at[c], req_rs.at[c], {"dom": to(c)})
        ask.start()
        asks.append(ask)

    for load in loads[1:]:
        load.wait()
    emb_parts = parts_of(emb_ref[...], 2)
    pairs, counts = pair_counts(src_ref, dst_ref, neg_ref, slots)

    ids = req_send[me]
    for c in range(1, ndom):
        asks[c - 1].wait_recv()
        ids = ids + req_recv[c]
    ids_all[rep] = ids

    row_id = lax.broadcasted_iota(jnp.int32, (slots, rows), 1)

    def hot_rows(row):
        return hot(row_id == jnp.broadcast_to(row, (8, slots)).T[:, 0:1])

    wanted = hot_rows(ids)
    pulled = mm_nt(wanted, emb_parts[0]) + mm_nt(wanted, emb_parts[1])
    pull_send[...] = pulled.reshape(ndom, capacity, width)
    def pull(k, worker):
        def copy(u, live):
            return remote(pull_send.at[worker, live], buf.at[me, live], pull_ss.at[k, u], pull_rs.at[k, u], {"dom": worker})
        return copy

    for k in range(1, ndom):
        units(me, to(k), lambda u, live: pull(k, to(k))(u, live).start())
    buf[me] = pull_send[me]
    tells = []
    for k in range(1, nrep):
        tell = remote(ids_all.at[rep], ids_all.at[rep], ids_ss.at[k], ids_rs.at[k], {"rep": rep_peer(k)})
        tell.start()
        tells.append(tell)

    for k in range(1, ndom):
        def landed(u, live):
            block = buf.at[source(k), live]
            remote(block, block, pull_ss.at[k, u], pull_rs.at[k, u], {"dom": source(k)}).wait_recv()
        units(source(k), me, landed)
    high, low = parts_of(buf[...].reshape(slots, width), 2)
    crossed = mm_nt(jnp.concatenate([high, low], axis=0), high)
    gram = crossed[:slots] + (crossed[slots:] + crossed[slots:].T)
    mixed = pairs * jax.nn.sigmoid(gram) - counts * jax.nn.sigmoid(-gram)
    mixed_high, mixed_low = parts_of(mixed, 2)
    gradient = mm(mixed_high, high) + (mm(mixed_high, low) + mm(mixed_low, high))
    grad_send[...] = gradient.reshape(ndom, capacity, width)

    def back(k, owner):
        def copy(u, live):
            return remote(grad_send.at[owner, live], grad_recv.at[rep, me, live], ret_ss.at[k, u], ret_rs.at[k, u], {"dom": owner})
        return copy

    for k in range(1, ndom):
        units(to(k), me, lambda u, live: back(k, to(k))(u, live).start())
    grad_recv[rep, me] = grad_send[me]

    direct = [2, 1] if relay else list(range(1, nrep))

    def share(g, k, p, peer):
        def copy(u, live):
            block = grad_recv.at[g, source(k), live]
            return remote(block, block, rep_ss.at[p, k, u], rep_rs.at[p, k, u], {"rep": peer})
        return copy

    for k in range(ndom):
        def pass_on(u, live):
            if k > 0:
                block = grad_recv.at[rep, source(k), live]
                remote(block, block, ret_ss.at[k, u], ret_rs.at[k, u], {"dom": source(k)}).wait_recv()
            for p in direct:
                share(rep, k, p, rep_peer(p))(u, live).start()
        units(me, source(k), pass_on)

    for tell in tells:
        tell.wait_recv()

    def arrived(p, k, then=None):
        def wait(u, live):
            share(rep_peer(p), k, p, rep_peer(p))(u, live).wait_recv()
            if then is not None:
                then(u, live)
        units(me, source(k), wait)

    def half_sum(half, first):
        groups = max(nrep // 2, 1)
        total = jnp.zeros((width, rows), F32)
        hots = [hot_rows(ids_all[first + g]) for g in range(groups)]
        stacked = jnp.concatenate(hots, axis=0)
        data = grad_recv[pl.ds(first, groups)].reshape(groups * slots, width)
        for part in parts_of(data, 2):
            total += lax.dot_general(part, stacked, (((0,), (0,)), ((), ())), preferred_element_type=F32)
        halves[half] = total

    if relay:
        chip = rep // 2
        for k in range(ndom):
            arrived(1, k)
        half_sum(chip, 2 * chip)
        for k in range(ndom):
            arrived(2, k, lambda u, live: share(rep_peer(2), k, 3, rep_peer(1))(u, live).start())
        for k in range(ndom):
            arrived(3, k)
        half_sum(1 - chip, 2 - 2 * chip)
    else:
        for p in direct:
            for k in range(ndom):
                arrived(p, k)
        half_sum(0, 0)
        half_sum(1, nrep // 2)
    total_out[...] = halves[0] + halves[1]

    for copy in asks + tells:
        copy.wait_send()
    for k in range(ndom):
        if k > 0:
            units(me, to(k), lambda u, live: pull(k, to(k))(u, live).wait_send())
            units(to(k), me, lambda u, live: back(k, to(k))(u, live).wait_send())
        for p in direct:
            units(me, source(k), lambda u, live: share(rep, k, p, rep_peer(p))(u, live).wait_send())
        if relay:
            units(me, source(k), lambda u, live: share(rep_peer(2), k, 3, rep_peer(1))(u, live).wait_send())


def adagrad(total_ref, emb_ref, sum_ref, rows_out, sum_out):
    row_grad = total_ref[...]
    width = row_grad.shape[0]
    new_sum = sum_ref[...] + jnp.sum(row_grad * row_grad, axis=0, keepdims=True) * (1.0 / width)
    sum_out[...] = new_sum
    rows_out[...] = emb_ref[...] - row_grad * (learn_rate / jnp.sqrt(new_sum))


def local(ndom, nrep, embedding, adagrad_sum, row_lists, source_slots, target_slots, negative_ids):
    rows, width = embedding.shape
    capacity = row_lists.shape[3]
    slots = ndom * capacity
    dma = pltpu.SemaphoreType.DMA
    vmem = pl.BlockSpec(memory_space=pltpu.VMEM)
    table = embedding.T
    total = pl.pallas_call(
        functools.partial(kernel, ndom, nrep),
        out_shape=jax.ShapeDtypeStruct((width, rows), F32),
        in_specs=[pl.BlockSpec(memory_space=pltpu.HBM)] * 5,
        out_specs=vmem,
        scratch_shapes=[
            pltpu.VMEM((width, rows), F32),
            pltpu.VMEM(row_lists.shape, jnp.int32),
            pltpu.VMEM(source_slots.shape, jnp.int32),
            pltpu.VMEM(target_slots.shape, jnp.int32),
            pltpu.VMEM(negative_ids.shape, jnp.int32),
            pltpu.VMEM((ndom, 1, slots), jnp.int32),
            pltpu.VMEM((ndom, 1, slots), jnp.int32),
            pltpu.VMEM((ndom, capacity, width), F32),
            pltpu.VMEM((ndom, capacity, width), F32),
            pltpu.VMEM((ndom, capacity, width), F32),
            pltpu.VMEM((nrep, ndom, capacity, width), F32),
            pltpu.VMEM((nrep, 1, slots), jnp.int32),
            pltpu.VMEM((2, width, rows), F32),
            dma((5,)),
            dma((ndom,)), dma((ndom,)), dma((ndom, 2)), dma((ndom, 2)), dma((ndom, 2)), dma((ndom, 2)),
            dma((nrep, ndom, 2)), dma((nrep, ndom, 2)), dma((nrep,)), dma((nrep,)),
        ],
        compiler_params=pltpu.CompilerParams(
            collective_id=0, has_side_effects=True, vmem_limit_bytes=60 << 20
        ),
    )(table, row_lists, source_slots, target_slots, negative_ids)
    steps = 2 if rows % 256 == 0 else 1
    block = pl.BlockSpec((width, rows // steps), lambda i: (0, i))
    line = pl.BlockSpec((1, rows // steps), lambda i: (0, i))
    new_rows, new_sum = pl.pallas_call(
        adagrad,
        out_shape=(jax.ShapeDtypeStruct((width, rows), F32), jax.ShapeDtypeStruct((1, rows), F32)),
        grid=(steps,),
        in_specs=[block, block, line],
        out_specs=(block, line),
        compiler_params=pltpu.CompilerParams(vmem_limit_bytes=60 << 20),
    )(total, table, adagrad_sum.reshape(1, rows))
    return (new_rows.T, new_sum.reshape(rows))


def solution(mesh):
    in_specs = (
        P("dom", None),
        P("dom"),
        P("rep", "dom", None, None),
        P("rep", "dom", None, None),
        P("rep", "dom", None, None),
        P("rep", "dom", None, None, None),
    )
    out_specs = (P("dom", None), P("dom"))
    body = functools.partial(local, mesh.shape["dom"], mesh.shape["rep"])
    return jax.shard_map(body, mesh=mesh, in_specs=in_specs, out_specs=out_specs, check_vma=False)
```

time: 31.9 us -> 31.7 us (level)
  local copies, waits for them, and re-layouts: 2.67 us -> 0 us
  Pallas kernels: 28.5 us -> 30.9 us
    unnamed x4 -> x0, local copies, waits for them, and re-layouts: 2.67 us -> none
    pallas_call x1 -> x2, Pallas kernels: 28.5 us -> 30.9 us  [the longest x1 28.6 us: local(): pl.pallas_call(functools.partial(kernel, ndom, nrep), out_shape=jax.Shape...]
where the time goes in v4:
time: 31.7 us; the launch traced here: 31.6 us
  Pallas kernels  30.9 us (97%)
  between operations  0.64 us (2%)
    pallas_call x1, Pallas kernels, local(): pl.pallas_call(functools.partial(kernel, ndom, nrep), out_shape=jax.Shape...  28.6 us
    pallas_call x1, Pallas kernels, local(): pl.pallas_call(adagrad, out_shape=(jax.ShapeDtypeStruct((width, rows), F3...  2.29 us

profile of v4, /device:TPU:1, one launch (start us, length us, event | category | flops | bytes accessed | tf_op | source)
XLA Modules:
  0.0 31.6 jit_solution(16584906560755032711)
XLA Ops:
  0.6 28.6 %shard_map.77.total_ref = f32[400,512]{1,0:T(8,128)} custom-call(f32[400,512]{1,0:T(8,128)} %bitcast.4, s32[1,1,8,16]{3,2,1,0:T(8,128)} %lists_hbm.1, s32[1,1,2,512]{3,2,1,0:T(2,128)} %src_hbm.1, s32[1,1,2,512]{3,2,1,0:T(2,128)} %dst_hbm.1, s32[1,1,2,2,512]{4,3,2,1,0:T(2,128)} %neg_hbm.1), custom_call_target="tpu_custom_call" | custom-call | tf_op jit(solution)/shard_map/pallas_call | solution.py:284
  29.3 2.3 %shard_map.78 = (f32[400,512]{1,0:T(8,128)}, f32[1,512]{1,0:T(1,128)}) custom-call(f32[400,512]{1,0:T(8,128)} %shard_map.77.total_ref, f32[400,512]{1,0:T(8,128)} %bitcast.5, f32[1,512]{1,0:T(1,128)} %bitcast.6), custom_call_target="tpu_custom_call" | custom-call | tf_op jit(solution)/shard_map/pallas_call | solution.py:314

commit v5 on v4

--- a/solution.py
+++ b/solution.py
@@ -36,26 +36,31 @@
     return mask.astype(F32).astype(BF)
 
 
-def pair_counts(src_ref, dst_ref, neg_ref, slots):
-    batches, edges = src_ref.shape[2:]
+def pair_counts(batches, src_ref, dst_ref, neg_ref, slots):
+    edges = src_ref.shape[3]
     samples = neg_ref.shape[4]
+    groups = -(-edges // 128)
     slot_id = lax.broadcasted_iota(jnp.int32, (slots, edges), 0)
-    edge_id = lax.broadcasted_iota(jnp.int32, (edges, samples), 0)
-    ones = jnp.ones((8, samples), BF)
+    lane_id = lax.broadcasted_iota(jnp.int32, (128, samples), 0)
+    group_id = lax.broadcasted_iota(jnp.int32, (-(-groups // 8) * 8, samples), 0)
     pairs = jnp.zeros((slots, slots), F32)
     counts = jnp.zeros((slots, slots), F32)
-    for b in range(batches):
+    for b in batches:
         src_mask = (slot_id == src_ref[0, 0, b : b + 1, :]).astype(F32)
         dst_mask = (slot_id == dst_ref[0, 0, b : b + 1, :]).astype(F32)
         src_hot = src_mask.astype(BF)
         dst_hot = dst_mask.astype(BF)
         counts += mm_nt(src_hot, dst_hot)
         for side, (near, far) in enumerate(((src_mask, dst_hot), (dst_mask, src_hot))):
-            chosen = hot(edge_id == neg_ref[0, 0, b, side : side + 1, :])
-            negative = mm(far, chosen).astype(BF)
-            times = mm_nt(ones, negative)[0:1, :]
+            drawn = neg_ref[0, 0, b, side : side + 1, :]
+            in_lane = hot(lane_id == jnp.bitwise_and(drawn, 127))
+            in_group = hot(group_id == lax.shift_right_logical(drawn, jnp.full_like(drawn, 7)))
+            table = mm_nt(in_group, in_lane)
+            drawn_times = jnp.concatenate([table[g : g + 1] for g in range(groups)], axis=1)[:, :edges]
+            drawn_high, drawn_low = parts_of(jnp.broadcast_to(drawn_times, (8, edges)), 2)
+            times = (mm_nt(drawn_high, far) + mm_nt(drawn_low, far))[0:1, :]
             pairs += jnp.sum(near, axis=1, keepdims=True) * times
-    return (pairs + pairs.T) * (1.0 / samples), counts + counts.T
+    return pairs, counts
 
 
 def kernel(
@@ -147,7 +152,8 @@
     for load in loads[1:]:
         load.wait()
     emb_parts = parts_of(emb_ref[...], 2)
-    pairs, counts = pair_counts(src_ref, dst_ref, neg_ref, slots)
+    batches = range(src_ref.shape[2])
+    pairs, counts = pair_counts(batches[:1], src_ref, dst_ref, neg_ref, slots)
 
     ids = req_send[me]
     for c in range(1, ndom):
@@ -176,6 +182,11 @@
         tell = remote(ids_all.at[rep], ids_all.at[rep], ids_ss.at[k], ids_rs.at[k], {"rep": rep_peer(k)})
         tell.start()
         tells.append(tell)
+
+    more_pairs, more_counts = pair_counts(batches[1:], src_ref, dst_ref, neg_ref, slots)
+    pairs, counts = pairs + more_pairs, counts + more_counts
+    pairs = (pairs + pairs.T) * (1.0 / neg_ref.shape[4])
+    counts = counts + counts.T
 
     for k in range(1, ndom):
         def landed(u, live):
@@ -199,6 +210,16 @@
         units(to(k), me, lambda u, live: back(k, to(k))(u, live).start())
     grad_recv[rep, me] = grad_send[me]
 
+    for tell in tells:
+        tell.wait_recv()
+    groups = max(nrep // 2, 1)
+    near_half = rep // 2 if relay else 0
+    far_half = 1 - near_half
+    owned = [
+        jnp.concatenate([hot_rows(ids_all[groups * half + g]) for g in range(groups)], axis=0)
+        for half in (near_half, far_half)
+    ]
+
     direct = [2, 1] if relay else list(range(1, nrep))
 
     def share(g, k, p, peer):
@@ -216,8 +237,6 @@
                 share(rep, k, p, rep_peer(p))(u, live).start()
         units(me, source(k), pass_on)
 
-    for tell in tells:
-        tell.wait_recv()
 
     def arrived(p, k, then=None):
         def wait(u, live):
@@ -226,32 +245,28 @@
                 then(u, live)
         units(me, source(k), wait)
 
-    def half_sum(half, first):
-        groups = max(nrep // 2, 1)
+    def half_sum(half, stacked):
         total = jnp.zeros((width, rows), F32)
-        hots = [hot_rows(ids_all[first + g]) for g in range(groups)]
-        stacked = jnp.concatenate(hots, axis=0)
-        data = grad_recv[pl.ds(first, groups)].reshape(groups * slots, width)
+        data = grad_recv[pl.ds(groups * half, groups)].reshape(groups * slots, width)
         for part in parts_of(data, 2):
             total += lax.dot_general(part, stacked, (((0,), (0,)), ((), ())), preferred_element_type=F32)
         halves[half] = total
 
     if relay:
-        chip = rep // 2
         for k in range(ndom):
             arrived(1, k)
-        half_sum(chip, 2 * chip)
+        half_sum(near_half, owned[0])
         for k in range(ndom):
             arrived(2, k, lambda u, live: share(rep_peer(2), k, 3, rep_peer(1))(u, live).start())
         for k in range(ndom):
             arrived(3, k)
-        half_sum(1 - chip, 2 - 2 * chip)
+        half_sum(far_half, owned[1])
     else:
         for p in direct:
             for k in range(ndom):
                 arrived(p, k)
-        half_sum(0, 0)
-        half_sum(1, nrep // 2)
+        half_sum(near_half, owned[0])
+        half_sum(far_half, owned[1])
     total_out[...] = halves[0] + halves[1]
 
     for copy in asks + tells:

time: 31.7 us -> 31.6 us (level)
  no operation moved by 1% of the time
where the time goes in v5:
time: 31.6 us; the launch traced here: 31.5 us
  Pallas kernels  30.8 us (97%)
  between operations  0.64 us (2%)
    pallas_call x1, Pallas kernels, local(): pl.pallas_call(functools.partial(kernel, ndom, nrep), out_shape=jax.Shape...  28.5 us
    pallas_call x1, Pallas kernels, local(): pl.pallas_call(adagrad, out_shape=(jax.ShapeDtypeStruct((width, rows), F3...  2.29 us

profile of v5, /device:TPU:1, one launch (start us, length us, event | category | flops | bytes accessed | tf_op | source)
XLA Modules:
  0.0 31.5 jit_solution(6480315046990590228)
XLA Ops:
  0.6 28.5 %shard_map.77.total_ref = f32[400,512]{1,0:T(8,128)} custom-call(f32[400,512]{1,0:T(8,128)} %bitcast.4, s32[1,1,8,16]{3,2,1,0:T(8,128)} %lists_hbm.1, s32[1,1,2,512]{3,2,1,0:T(2,128)} %src_hbm.1, s32[1,1,2,512]{3,2,1,0:T(2,128)} %dst_hbm.1, s32[1,1,2,2,512]{4,3,2,1,0:T(2,128)} %neg_hbm.1), custom_call_target="tpu_custom_call" | custom-call | tf_op jit(solution)/shard_map/pallas_call | solution.py:299
  29.2 2.3 %shard_map.78 = (f32[400,512]{1,0:T(8,128)}, f32[1,512]{1,0:T(1,128)}) custom-call(f32[400,512]{1,0:T(8,128)} %shard_map.77.total_ref, f32[400,512]{1,0:T(8,128)} %bitcast.5, f32[1,512]{1,0:T(1,128)} %bitcast.6), custom_call_target="tpu_custom_call" | custom-call | tf_op jit(solution)/shard_map/pallas_call | solution.py:329
